TPU v7x, 32 devices: a whole 2x2x4 slice. The times are simulated.
32 devices in a mesh: outer: 4 (over z), inner: 2 (over x), chan: 4 (over y, core).
Axes of the slice: x: 2, y: 2, z: 4, core: 2. Of those that a mesh axis runs over, the one named last changes fastest.
Arguments:
- gate_proj: bfloat16 [128, 65536], P('chan', ('outer', 'inner')), may hold values from -6 to 6
- key_proj: bfloat16 [128, 65536], P('chan', ('outer', 'inner')), may hold values from -6 to 6
- value_proj: bfloat16 [128, 65536], P('chan', ('outer', 'inner')), may hold values from -6 to 6
- filter_taps: float32 [65536], P(('outer', 'inner', 'chan')), may hold values from -1 to 1, as said below
- skip_gain: float32 [128], P('chan'), may hold values from 0.5 to 1.5
Outputs:
- hyena_out: float32 [128, 65536], P('chan', ('outer', 'inner'))
Inputs may be any that keep to these rules, and one draw needn't show every extreme that they name: `filter_taps`: one filter for all 128 channels.
All inputs are finite; a program needn't handle non-finite values.
Results may differ from a plain program's by a relative error of at most 0.0003.
Values sent between devices are 32-bit elements; how exact they have to be, the bound alone decides.
A program may use at most 128 MiB of HBM per device.

v0:
```python
import functools
import math

import jax
import jax.numpy as jnp
import numpy as np
from jax import lax
from jax.experimental import pallas as pl
from jax.experimental.pallas import tpu as pltpu
from jax.sharding import PartitionSpec as P

HIGHEST = lax.Precision.HIGHEST


def count_up(length):
    return jnp.arange(length, dtype=jnp.int32)


def unit_table(row_index, col_index, modulus):
    turns = row_index * col_index % modulus
    angles = turns.astype(jnp.float32) * (2.0 * math.pi / modulus)
    return (jnp.cos(angles), jnp.sin(angles))


def multiply(form, left, right):
    return jnp.einsum(form, left, right, precision=HIGHEST)


def turn_forward(real_in, imag_in, cos_tab, sine_tab):
    return (real_in * cos_tab + imag_in * sine_tab, imag_in * cos_tab - real_in * sine_tab)


def turn_backward(real_in, imag_in, cos_tab, sine_tab):
    return (real_in * cos_tab - imag_in * sine_tab, imag_in * cos_tab + real_in * sine_tab)


def column_forward(columns, groups, here, total_len):
    span = columns.shape[2]
    cos_m, sine_m = unit_table(count_up(2 * groups)[:, None], count_up(groups)[None, :], 2 * groups)
    real_col = multiply("am,cmr->car", cos_m, columns)
    imag_col = -multiply("am,cmr->car", sine_m, columns)
    positions = here * span + count_up(span)
    cos_r, sine_r = unit_table(count_up(2 * groups)[:, None], positions[None, :], total_len)
    return turn_forward(real_col, imag_col, cos_r, sine_r)


def column_forward_pair(real_cols, imag_cols, groups, here, total_len):
    span = real_cols.shape[2]
    cos_m, sine_m = unit_table(count_up(2 * groups)[:, None], count_up(groups)[None, :], 2 * groups)
    form = "am,cmr->car"
    real_col = multiply(form, cos_m, real_cols) + multiply(form, sine_m, imag_cols)
    imag_col = multiply(form, cos_m, imag_cols) - multiply(form, sine_m, real_cols)
    positions = here * span + count_up(span)
    cos_r, sine_r = unit_table(count_up(2 * groups)[:, None], positions[None, :], total_len)
    return turn_forward(real_col, imag_col, cos_r, sine_r)


def local_forward(real_in, imag_in):
    lead, pair, block_len = real_in.shape
    inner_len = 128
    outer_len = block_len // inner_len
    real_in = real_in.reshape(lead, pair, outer_len, inner_len)
    imag_in = imag_in.reshape(lead, pair, outer_len, inner_len)
    cos_a, sine_a = unit_table(
        count_up(outer_len)[:, None], count_up(outer_len)[None, :], outer_len
    )
    form_a = "jk,ceks->cejs"
    real_mid = multiply(form_a, cos_a, real_in) + multiply(form_a, sine_a, imag_in)
    imag_mid = multiply(form_a, cos_a, imag_in) - multiply(form_a, sine_a, real_in)
    cos_t, sine_t = unit_table(
        count_up(outer_len)[:, None], count_up(inner_len)[None, :], block_len
    )
    real_mid, imag_mid = turn_forward(real_mid, imag_mid, cos_t, sine_t)
    cos_b, sine_b = unit_table(
        count_up(inner_len)[:, None], count_up(inner_len)[None, :], inner_len
    )
    form_b = "cejs,st->cejt"
    real_out = multiply(form_b, real_mid, cos_b) + multiply(form_b, imag_mid, sine_b)
    imag_out = multiply(form_b, imag_mid, cos_b) - multiply(form_b, real_mid, sine_b)
    return (real_out, imag_out)


def local_backward(real_in, imag_in):
    lead, pair, outer_len, inner_len = real_in.shape
    block_len = outer_len * inner_len
    cos_b, sine_b = unit_table(
        count_up(inner_len)[:, None], count_up(inner_len)[None, :], inner_len
    )
    form_b = "cejt,st->cejs"
    real_mid = multiply(form_b, real_in, cos_b) - multiply(form_b, imag_in, sine_b)
    imag_mid = multiply(form_b, imag_in, cos_b) + multiply(form_b, real_in, sine_b)
    cos_t, sine_t = unit_table(
        count_up(outer_len)[:, None], count_up(inner_len)[None, :], block_len
    )
    real_mid, imag_mid = turn_backward(real_mid, imag_mid, cos_t, sine_t)
    cos_a, sine_a = unit_table(
        count_up(outer_len)[:, None], count_up(outer_len)[None, :], outer_len
    )
    form_a = "jk,cejs->ceks"
    real_out = multiply(form_a, cos_a, real_mid) - multiply(form_a, sine_a, imag_mid)
    imag_out = multiply(form_a, cos_a, imag_mid) + multiply(form_a, sine_a, real_mid)
    return (real_out.reshape(lead, pair, block_len), imag_out.reshape(lead, pair, block_len))


def local_columns(gate_proj, key_proj, value_proj, filter_taps, skip_gain):
    outer_count = lax.axis_size("outer")
    inner_count = lax.axis_size("inner")
    groups = outer_count * inner_count
    here = lax.axis_index(("outer", "inner"))
    chans, tok_local = gate_proj.shape
    half_chans = chans // 2
    span = tok_local // groups
    total_len = 2 * groups * tok_local
    signal = key_proj.astype(jnp.float32) * value_proj.astype(jnp.float32)
    taps_local = lax.all_gather(filter_taps, "chan", axis=0, tiled=True)
    sig_cols, tap_cols = (
        lax.all_to_all(
            signal.reshape(chans, groups, span),
            ("outer", "inner"),
            split_axis=1,
            concat_axis=1,
            tiled=True,
        ),
        lax.all_to_all(
            taps_local.reshape(1, groups, span),
            ("outer", "inner"),
            split_axis=1,
            concat_axis=1,
            tiled=True,
        ),
    )
    sig_real, sig_imag = column_forward_pair(
        sig_cols[:half_chans], sig_cols[half_chans:], groups, here, total_len
    )
    tap_real, tap_imag = column_forward(tap_cols, groups, here, total_len)
    sig_real, sig_imag, tap_real, tap_imag = (
        lax.all_to_all(sig_real, ("outer", "inner"), split_axis=1, concat_axis=2, tiled=True),
        lax.all_to_all(sig_imag, ("outer", "inner"), split_axis=1, concat_axis=2, tiled=True),
        lax.all_to_all(tap_real, ("outer", "inner"), split_axis=1, concat_axis=2, tiled=True),
        lax.all_to_all(tap_imag, ("outer", "inner"), split_axis=1, concat_axis=2, tiled=True),
    )
    sig_real, sig_imag = local_forward(sig_real, sig_imag)
    tap_real, tap_imag = local_forward(tap_real, tap_imag)
    prod_real = sig_real * tap_real - sig_imag * tap_imag
    prod_imag = sig_real * tap_imag + sig_imag * tap_real
    back_real, back_imag = local_backward(prod_real, prod_imag)
    back_real, back_imag = (
        lax.all_to_all(back_real, ("outer", "inner"), split_axis=2, concat_axis=1, tiled=True),
        lax.all_to_all(back_imag, ("outer", "inner"), split_axis=2, concat_axis=1, tiled=True),
    )
    positions = here * span + count_up(span)
    cos_r, sine_r = unit_table(count_up(2 * groups)[:, None], positions[None, :], total_len)
    back_real, back_imag = turn_backward(back_real, back_imag, cos_r, sine_r)
    cos_m, sine_m = unit_table(count_up(2 * groups)[:, None], count_up(groups)[None, :], 2 * groups)
    form_m = "am,car->cmr"
    conv_real = multiply(form_m, cos_m, back_real) - multiply(form_m, sine_m, back_imag)
    conv_imag = multiply(form_m, cos_m, back_imag) + multiply(form_m, sine_m, back_real)
    conv_cols = jnp.concatenate((conv_real, conv_imag), axis=0)
    conv_cols = conv_cols * (1.0 / total_len)
    conv = lax.all_to_all(
        conv_cols, ("outer", "inner"), split_axis=1, concat_axis=2, tiled=True
    ).reshape(chans, tok_local)
    return gate_proj.astype(jnp.float32) * (conv + skip_gain[:, None] * signal)


LANES = 128
COLS = 256
MESH = pl.DeviceIdType.MESH


def split_np(table):
    high = table.astype(jnp.bfloat16)
    low = (table - high.astype(np.float64)).astype(jnp.bfloat16)
    return np.stack((high, low))


@functools.lru_cache(maxsize=None)
def dft_tables(rows):
    freqs = 2 * rows
    total_len = freqs * COLS
    angle_a = np.outer(np.arange(freqs), np.arange(freqs)) % freqs * (2.0 * np.pi / freqs)
    cos_a, sine_a = np.cos(angle_a), np.sin(angle_a)
    angle_b = np.outer(np.arange(COLS), np.arange(COLS)) % COLS * (2.0 * np.pi / COLS)
    cos_b, sine_b = np.cos(angle_b), np.sin(angle_b)
    angle_t = np.outer(np.arange(freqs), np.arange(COLS)) * (2.0 * np.pi / total_len)
    return (
        split_np(np.concatenate((cos_a[:, :rows], sine_a[:, :rows]), axis=1)),
        split_np(np.concatenate((cos_a[:rows], sine_a[:rows]), axis=1)),
        split_np(np.block([[cos_b, -sine_b], [sine_b, cos_b]])),
        np.stack((np.cos(angle_t), np.sin(angle_t))).astype(np.float32),
    )


def split(value):
    high = value.astype(jnp.bfloat16)
    return high, (value - high.astype(jnp.float32)).astype(jnp.bfloat16)


def dot(left, right, dims=((1,), (0,))):
    return lax.dot_general(left, right, (dims, ((), ())), preferred_element_type=jnp.float32)


def dot3(left_hi, left_lo, right_hi, right_lo, dims=((1,), (0,))):
    return (
        dot(left_lo, right_hi, dims) + dot(left_hi, right_lo, dims) + dot(left_hi, right_hi, dims)
    )


def conv_kernel(
    sizes,
    sig_ref,
    tap_ref,
    fwd_hbm,
    inv_hbm,
    col_hbm,
    twid_hbm,
    conv_ref,
    xbuf,
    hbuf,
    ybuf,
    rhs,
    back,
    spec,
    fwd,
    inv,
    col,
    twid,
    sig_send,
    sig_recv,
    out_send,
    out_recv,
    tap_send,
    tap_recv,
    spread_send,
    spread_recv,
    own_sem,
    table_sem,
):
    outer_n, inner_n, chan_n = sizes
    groups = outer_n * inner_n
    mine_n = xbuf.shape[0]
    pairs = mine_n // 2
    rows = xbuf.shape[2]
    piece = rows // groups
    freqs = 2 * rows
    step = 256
    outer = lax.axis_index("outer")
    inner = lax.axis_index("inner")
    chan = lax.axis_index("chan")
    here = outer * inner_n + inner
    far = sorted(range(outer_n), key=lambda dz: -min(dz, outer_n - dz))
    hops = [(dz, dx) for dz in far for dx in reversed(range(inner_n)) if dz or dx]
    peers = []
    for dz, dx in hops:
        to_z = lax.rem(outer + dz, outer_n)
        to_x = lax.rem(inner + dx, inner_n)
        peers.append((to_z * inner_n + to_x, (to_z, to_x, chan)))
    sides = [(outer, inner, lax.rem(chan + dc, chan_n)) for dc in range(1, chan_n)]

    barrier = pltpu.get_barrier_semaphore()
    for _, where in peers:
        pl.semaphore_signal(barrier, inc=1, device_id=where, device_id_type=MESH)
    for where in sides:
        pl.semaphore_signal(barrier, inc=1, device_id=where, device_id_type=MESH)
    pl.semaphore_wait(barrier, len(peers) + len(sides))

    def remote(src, dst, send, recv, where):
        copy = pltpu.make_async_remote_copy(
            src_ref=src,
            dst_ref=dst,
            send_sem=send,
            recv_sem=recv,
            device_id=where,
            device_id_type=MESH,
        )
        copy.start()
        return copy

    tap_copies = [
        remote(tap_ref, hbuf.at[:, here, chan], tap_send.at[j], tap_recv.at[j], where)
        for j, (_, where) in enumerate(peers)
    ]
    own = [pltpu.make_async_copy(tap_ref, hbuf.at[:, here, chan], own_sem.at[2 * pairs])]
    own[0].start()
    sig_copies = []
    for pair in range(pairs):
        sig_copies.append(
            [
                remote(
                    sig_ref.at[pl.ds(dest * mine_n + 2 * pair, 2)],
                    xbuf.at[pl.ds(2 * pair, 2), :, pl.ds(here * piece, piece)],
                    sig_send.at[pair, j],
                    sig_recv.at[pair, j],
                    where,
                )
                for j, (dest, where) in enumerate(peers)
            ]
        )
    for pair in range(pairs):
        keep = pltpu.make_async_copy(
            sig_ref.at[pl.ds(here * mine_n + 2 * pair, 2)],
            xbuf.at[pl.ds(2 * pair, 2), :, pl.ds(here * piece, piece)],
            own_sem.at[pair],
        )
        keep.start()
        own.append(keep)
    tables = [
        pltpu.make_async_copy(src, dst, table_sem.at[i])
        for i, (src, dst) in enumerate(
            ((fwd_hbm, fwd), (col_hbm, col), (twid_hbm, twid), (inv_hbm, inv))
        )
    ]
    for copy in tables:
        copy.start()

    own[0].wait()
    for copy in tap_copies:
        copy.wait_recv()
    spread_copies = [
        remote(hbuf.at[:, :, chan], hbuf.at[:, :, chan], spread_send.at[j], spread_recv.at[j], where)
        for j, where in enumerate(sides)
    ]
    for copy in tables:
        copy.wait()
    for copy in spread_copies:
        copy.wait_recv()

    def fill(real, imag):
        for half in range(2):
            for part, at, sign in (
                (real, (0, 0), 1.0),
                (imag, (0, 1), 1.0),
                (imag, (1, 0), 1.0),
                (real, (1, 1), -1.0),
            ):
                lanes = pl.ds(at[1] * COLS + half * LANES, LANES)
                if part is None:
                    high = low = jnp.zeros((rows, LANES), jnp.bfloat16)
                else:
                    high, low = split(sign * part(half))
                rhs[0, pl.ds(at[0] * rows, rows), lanes] = high
                rhs[1, pl.ds(at[0] * rows, rows), lanes] = low

    def forward(at):
        mid = dot3(fwd[0, at, :], fwd[1, at, :], rhs[0], rhs[1])
        real, imag = mid[:, :COLS], mid[:, COLS:]
        cos_t, sine_t = twid[0, at, :], twid[1, at, :]
        turned = jnp.concatenate(turn_forward(real, imag, cos_t, sine_t), axis=1)
        return dot3(*split(turned), col[0], col[1])

    fill(lambda half: hbuf[half].reshape(rows, LANES), None)

    def filter_step(t, carry):
        at = pl.ds(pl.multiple_of(t * step, step), step)
        spec[at, :] = forward(at) * (1.0 / (freqs * COLS))
        return carry

    lax.fori_loop(0, freqs // step, filter_step, 0)

    out_copies = []
    for pair in range(pairs):
        own[1 + pair].wait()
        for copy in sig_copies[pair]:
            copy.wait_recv()
        fill(lambda half: xbuf[2 * pair, half], lambda half: xbuf[2 * pair + 1, half])

        def pair_step(t, carry):
            at = pl.ds(pl.multiple_of(t * step, step), step)
            below = pl.ds(pl.multiple_of(t * step + freqs, step), step)
            freq = forward(at)
            real, imag = freq[:, :COLS], freq[:, COLS:]
            spec_real, spec_imag = spec[at, :COLS], spec[at, COLS:]
            prod = jnp.concatenate(
                (real * spec_real - imag * spec_imag, real * spec_imag + imag * spec_real), axis=1
            )
            mid = dot3(*split(prod), col[0], col[1], ((1,), (1,)))
            cos_t, sine_t = twid[0, at, :], twid[1, at, :]
            real, imag = turn_backward(mid[:, :COLS], mid[:, COLS:], cos_t, sine_t)
            real_hi, real_lo = split(real)
            imag_hi, imag_lo = split(imag)
            back[0, at, :COLS] = real_hi
            back[1, at, :COLS] = real_lo
            back[0, at, COLS:] = imag_hi
            back[1, at, COLS:] = imag_lo
            back[0, below, :COLS] = -imag_hi
            back[1, below, :COLS] = -imag_lo
            back[0, below, COLS:] = real_hi
            back[1, below, COLS:] = real_lo
            return carry

        lax.fori_loop(0, freqs // step, pair_step, 0)
        result = dot3(inv[0], inv[1], back[0], back[1])
        for which in range(2):
            for half in range(2):
                first = which * COLS + half * LANES
                ybuf[2 * pair + which, half] = result[:, first : first + LANES]
        out_copies.append(
            [
                remote(
                    ybuf.at[pl.ds(2 * pair, 2), :, pl.ds(dest * piece, piece)],
                    conv_ref.at[pl.ds(here * mine_n + 2 * pair, 2)],
                    out_send.at[pair, j],
                    out_recv.at[pair, j],
                    where,
                )
                for j, (dest, where) in enumerate(peers)
            ]
        )
        keep = pltpu.make_async_copy(
            ybuf.at[pl.ds(2 * pair, 2), :, pl.ds(here * piece, piece)],
            conv_ref.at[pl.ds(here * mine_n + 2 * pair, 2)],
            own_sem.at[pairs + pair],
        )
        keep.start()
        own.append(keep)

    for pair in range(pairs):
        own[1 + pairs + pair].wait()
        for copy in out_copies[pair]:
            copy.wait_recv()
    for copy in tap_copies + spread_copies + sum(sig_copies, []) + sum(out_copies, []):
        copy.wait_send()


def local_whole(gate_proj, key_proj, value_proj, filter_taps, skip_gain):
    sizes = tuple(lax.axis_size(name) for name in ("outer", "inner", "chan"))
    groups = sizes[0] * sizes[1]
    chans, tok_local = gate_proj.shape
    mine_n = chans // groups
    pairs = mine_n // 2
    piece = tok_local // COLS
    rows = groups * piece
    tap_rows = filter_taps.shape[0] // COLS
    signal = key_proj.astype(jnp.float32) * value_proj.astype(jnp.float32)
    sig_in = signal.reshape(chans, piece, 2, LANES).transpose(0, 2, 1, 3)
    tap_in = filter_taps.reshape(tap_rows, 2, LANES).transpose(1, 0, 2)
    dma = pltpu.SemaphoreType.DMA
    vmem = pl.BlockSpec(memory_space=pltpu.VMEM)
    hbm = pl.BlockSpec(memory_space=pl.ANY)
    tables = dft_tables(rows)
    conv = pl.pallas_call(
        functools.partial(conv_kernel, sizes),
        out_shape=jax.ShapeDtypeStruct((chans, 2, piece, LANES), jnp.float32),
        in_specs=[vmem, vmem, hbm, hbm, hbm, hbm],
        out_specs=vmem,
        scratch_shapes=[
            pltpu.VMEM((mine_n, 2, rows, LANES), jnp.float32),
            pltpu.VMEM((2, groups, sizes[2], tap_rows, LANES), jnp.float32),
            pltpu.VMEM((mine_n, 2, rows, LANES), jnp.float32),
            pltpu.VMEM((2, 2 * rows, 2 * COLS), jnp.bfloat16),
            pltpu.VMEM((2, 4 * rows, 2 * COLS), jnp.bfloat16),
            pltpu.VMEM((2 * rows, 2 * COLS), jnp.float32),
            pltpu.VMEM(tables[0].shape, jnp.bfloat16),
            pltpu.VMEM(tables[1].shape, jnp.bfloat16),
            pltpu.VMEM(tables[2].shape, jnp.bfloat16),
            pltpu.VMEM(tables[3].shape, jnp.float32),
            dma((pairs, groups - 1)),
            dma((pairs, groups - 1)),
            dma((pairs, groups - 1)),
            dma((pairs, groups - 1)),
            dma((groups - 1,)),
            dma((groups - 1,)),
            dma((sizes[2] - 1,)),
            dma((sizes[2] - 1,)),
            dma((2 * pairs + 1,)),
            dma((4,)),
        ],
        compiler_params=pltpu.CompilerParams(
            collective_id=0, has_side_effects=True, vmem_limit_bytes=48 * 1024 * 1024
        ),
    )(sig_in, tap_in, *(jnp.asarray(table) for table in tables))
    conv = conv.transpose(0, 2, 1, 3).reshape(chans, tok_local)
    return gate_proj.astype(jnp.float32) * (conv + skip_gain[:, None] * signal)


def local(gate_proj, key_proj, value_proj, filter_taps, skip_gain):
    groups = lax.axis_size("outer") * lax.axis_size("inner")
    whole_pairs = gate_proj.shape[0] % (2 * groups) == 0
    tiled = gate_proj.shape[1] % (8 * COLS) == 0 and filter_taps.shape[0] % (8 * COLS) == 0
    one = local_whole if whole_pairs and tiled else local_columns
    return one(gate_proj, key_proj, value_proj, filter_taps, skip_gain)


def solution(mesh):
    placed = (
        P("chan", ("outer", "inner")),
        P("chan", ("outer", "inner")),
        P("chan", ("outer", "inner")),
        P(("outer", "inner", "chan")),
        P("chan"),
    )
    return jax.shard_map(
        local, mesh=mesh, in_specs=placed, out_specs=P("chan", ("outer", "inner")), check_vma=False
    )
```

profile of v0, /device:TPU:0, one launch (start us, length us, event | category | flops | bytes accessed | tf_op | source)
XLA Modules:
  0.0 61.5 jit_solution(5791625448939361101)
XLA Ops:
  0.0 0.7 %copy.16 = f32[8,2,128]{2,0,1:T(8,128)S(1)} copy(f32[8,2,128]{2,1,0:T(2,128)} %bitcast.11) | data formatting | bytes 16384 | tf_op jit(solution)/shard_map/reshape | solution.py:436
  0.7 1.3 %convert_multiply_fusion = f32[32,8192]{1,0:T(8,128)S(1)} fusion(bf16[32,8192]{1,0:T(8,128)(2,1)} %param.11, bf16[32,8192]{1,0:T(8,128)(2,1)} %param.10), kind=kLoop, calls=%fused_computation.2 | loop fusion | flops 786432 | bytes 2097152 | tf_op jit(solution)/shard_map/mul | solution.py:434
  2.0 0.0 copy-start.2
  2.0 0.9 %reshape.10 = f32[32,32,2,128]{3,2,1,0:T(2,128)S(1)} reshape(f32[32,8192]{1,0:T(8,128)S(1)} %convert_multiply_fusion) | data formatting | bytes 2097152 | tf_op jit(solution)/shard_map/reshape | solution.py:435
  2.9 0.0 copy-start
  2.9 0.0 copy-start.1
  2.9 0.1 copy.15
  3.1 0.2 copy-done.2
  3.2 1.0 %copy-done = bf16[2,512,512]{2,1,0:T(8,128)(2,1)S(1)} copy-done((bf16[2,512,512]{2,1,0:T(8,128)(2,1)S(1)}, bf16[2,512,512]{2,1,0:T(8,128)(2,1)}, u32[]{:S(2)}) %copy-start) | copy-done | bytes 1048600
  4.2 0.3 copy-done.1
  4.5 52.6 %shard_map.91 = f32[32,2,32,128]{3,2,1,0:T(8,128)S(1)} custom-call(f32[32,2,32,128]{3,2,1,0:T(8,128)S(1)} %bitcast.8, f32[2,8,128]{2,1,0:T(8,128)S(1)} %bitcast.10, bf16[2,512,512]{2,1,0:T(8,128)(2,1)S(1)} %copy-done.2, bf16[2,256,1024]{2,1,0:T(8,128)(2,1)S(1)} %copy-done.1, bf16[2,512,512]{2,1,0:T(8,128)(2,1)S(1)} %copy-done, ...), custom_call_target="tpu_custom_call" | custom-call | tf_op jit(solution)/shard_map/pallas_call | solution.py:441
  57.2 0.8 %copy.12 = f32[32,32,2,128]{3,2,1,0:T(2,128)S(1)} copy(f32[32,32,2,128]{3,1,2,0:T(8,128)S(1)} %bitcast.9) | data formatting | bytes 2097152 | tf_op jit(solution)/shard_map/transpose | solution.py:472
  58.0 0.0 copy-start.3
  58.0 0.0 copy-start.4
  58.0 0.0 copy-start.5
  58.1 0.8 %reshape.12 = f32[32,8192]{1,0:T(8,128)S(1)} reshape(f32[32,32,2,128]{3,2,1,0:T(2,128)S(1)} %copy.12) | data formatting | bytes 2097152 | tf_op jit(solution)/shard_map/reshape | solution.py:472
  58.9 0.2 copy-done.3
  59.1 0.2 copy-done.4
  59.2 0.0 copy-done.5
  59.2 2.3 %add_multiply_fusion = f32[32,8192]{1,0:T(8,128)} fusion(f32[32,8192]{1,0:T(8,128)S(1)} %reshape.12, bf16[32,8192]{1,0:T(8,128)(2,1)} %param.9, f32[32]{0:T(128)S(1)} %copy-done.5, bf16[32,8192]{1,0:T(8,128)(2,1)S(1)} %copy-done.3, bf16[32,8192]{1,0:T(8,128)(2,1)S(1)} %copy-done.4), kind=kLoop, calls=%fused_computation.1 | loop fusion | flops 1835008 | bytes 3670144 | tf_op jit(solution)/shard_map/mul | solution.py:473
Async XLA Ops:
  2.0 1.2 %copy-start.2 = (bf16[2,512,512]{2,1,0:T(8,128)(2,1)S(1)}, bf16[2,512,512]{2,1,0:T(8,128)(2,1)}, u32[]{:S(2)}) copy-start(bf16[2,512,512]{2,1,0:T(8,128)(2,1)} %constant.8.clone.fwd_hbm) | copy-start | bytes 3145732
  2.9 1.3 %copy-start = (bf16[2,512,512]{2,1,0:T(8,128)(2,1)S(1)}, bf16[2,512,512]{2,1,0:T(8,128)(2,1)}, u32[]{:S(2)}) copy-start(bf16[2,512,512]{2,1,0:T(8,128)(2,1)} %constant.10.clone.col_hbm) | copy-start | bytes 3145732
  2.9 1.6 %copy-start.1 = (bf16[2,256,1024]{2,1,0:T(8,128)(2,1)S(1)}, bf16[2,256,1024]{2,1,0:T(8,128)(2,1)}, u32[]{:S(2)}) copy-start(bf16[2,256,1024]{2,1,0:T(8,128)(2,1)} %constant.9.clone.inv_hbm) | copy-start | bytes 3145732
  58.0 1.0 %copy-start.3 = (bf16[32,8192]{1,0:T(8,128)(2,1)S(1)}, bf16[32,8192]{1,0:T(8,128)(2,1)}, u32[]{:S(2)}) copy-start(bf16[32,8192]{1,0:T(8,128)(2,1)} %param.11) | copy-start | bytes 1572868
  58.0 1.2 %copy-start.4 = (bf16[32,8192]{1,0:T(8,128)(2,1)S(1)}, bf16[32,8192]{1,0:T(8,128)(2,1)}, u32[]{:S(2)}) copy-start(bf16[32,8192]{1,0:T(8,128)(2,1)} %param.10) | copy-start | bytes 1572868
  58.0 1.2 %copy-start.5 = (f32[32]{0:T(128)S(1)}, f32[32]{0:T(128)}, u32[]{:S(2)}) copy-start(f32[32]{0:T(128)} %param.13) | copy-start | bytes 388
where the time goes:
time: 61.8 us; the launch traced here: 61.5 us
  Pallas kernels  52.6 us (85%)
  local copies, waits for them, and re-layouts  5.2 us (8%)
  other arithmetic  3.57 us (6%)
    pallas_call x1, Pallas kernels, local_whole(): pl.pallas_call(functools.partial(conv_kernel, sizes), out_shape=jax.Shape...  52.6 us
    mul x1, other arithmetic, local_whole(): return gate_proj.astype(jnp.float32) * (conv + skip_gain[:, None] * signal)  2.27 us
    unnamed x12, local copies, waits for them, and re-layouts  1.81 us
    mul x1, other arithmetic, local_whole(): signal = key_proj.astype(jnp.float32) * value_proj.astype(jnp.float32)  1.3 us

commit v1 on v0

--- a/solution.py
+++ b/solution.py
@@ -206,15 +206,30 @@
     )
 
 
+def flip(index, bits):
+    for k in range(bits.bit_length()):
+        if bits >> k & 1:
+            index = index + (1 - 2 * (index // 2**k % 2)) * 2**k
+    return index
+
+
 def conv_kernel(
     sizes,
-    sig_ref,
+    gate_hbm,
+    key_hbm,
+    value_hbm,
     tap_ref,
+    skip_ref,
     fwd_hbm,
     inv_hbm,
     col_hbm,
     twid_hbm,
-    conv_ref,
+    out_ref,
+    gate,
+    key,
+    value,
+    sig,
+    conv,
     xbuf,
     hbuf,
     ybuf,
@@ -235,33 +250,51 @@
     spread_recv,
     own_sem,
     table_sem,
+    load_sem,
 ):
     outer_n, inner_n, chan_n = sizes
     groups = outer_n * inner_n
-    mine_n = xbuf.shape[0]
+    chans, tok_local = out_ref.shape
+    tiles = tok_local // LANES
+    mine_n = chans // groups
     pairs = mine_n // 2
-    rows = xbuf.shape[2]
-    piece = rows // groups
+    rows = groups * tiles // 2
     freqs = 2 * rows
     step = 256
     outer = lax.axis_index("outer")
     inner = lax.axis_index("inner")
     chan = lax.axis_index("chan")
     here = outer * inner_n + inner
-    far = sorted(range(outer_n), key=lambda dz: -min(dz, outer_n - dz))
-    hops = [(dz, dx) for dz in far for dx in reversed(range(inner_n)) if dz or dx]
+    hops = [(dz, dx) for dz in range(outer_n)[::-1] for dx in range(inner_n)[::-1] if dz or dx]
     peers = []
     for dz, dx in hops:
-        to_z = lax.rem(outer + dz, outer_n)
-        to_x = lax.rem(inner + dx, inner_n)
+        to_z, to_x = flip(outer, dz), flip(inner, dx)
         peers.append((to_z * inner_n + to_x, (to_z, to_x, chan)))
-    sides = [(outer, inner, lax.rem(chan + dc, chan_n)) for dc in range(1, chan_n)]
+    sides = [(outer, inner, flip(chan, dc)) for dc in range(1, chan_n)]
 
     barrier = pltpu.get_barrier_semaphore()
     for _, where in peers:
         pl.semaphore_signal(barrier, inc=1, device_id=where, device_id_type=MESH)
     for where in sides:
         pl.semaphore_signal(barrier, inc=1, device_id=where, device_id_type=MESH)
+
+    loads = [
+        pltpu.make_async_copy(src, dst, load_sem.at[k])
+        for k, (src, dst) in enumerate(((key_hbm, key), (value_hbm, value), (gate_hbm, gate)))
+    ]
+    for copy in loads:
+        copy.start()
+    loads[0].wait()
+    loads[1].wait()
+
+    def product_step(t, carry):
+        lanes = pl.ds(pl.multiple_of(t * LANES, LANES), LANES)
+        prod = key[:, lanes].astype(jnp.float32) * value[:, lanes].astype(jnp.float32)
+        for k in range(chans // 8):
+            sig[pl.ds(8 * k * tiles + t, 8, stride=tiles), :] = prod[8 * k : 8 * k + 8]
+        return carry
+
+    lax.fori_loop(0, tiles, product_step, 0, unroll=8)
     pl.semaphore_wait(barrier, len(peers) + len(sides))
 
     def remote(src, dst, send, recv, where):
@@ -276,31 +309,38 @@
         copy.start()
         return copy
 
+    def outside(ref, owner, which):
+        first = pl.multiple_of((owner * mine_n + which) * tiles, 8)
+        return ref.at[pl.ds(first, tiles)]
+
+    def inside(ref, place, which):
+        first = pl.multiple_of((which * groups + place) * tiles, 8)
+        return ref.at[pl.ds(first, tiles)]
+
     tap_copies = [
-        remote(tap_ref, hbuf.at[:, here, chan], tap_send.at[j], tap_recv.at[j], where)
+        remote(tap_ref, hbuf.at[here, chan], tap_send.at[j], tap_recv.at[j], where)
         for j, (_, where) in enumerate(peers)
     ]
-    own = [pltpu.make_async_copy(tap_ref, hbuf.at[:, here, chan], own_sem.at[2 * pairs])]
+    own = [pltpu.make_async_copy(tap_ref, hbuf.at[here, chan], own_sem.at[2 * mine_n])]
     own[0].start()
     sig_copies = []
     for pair in range(pairs):
         sig_copies.append(
             [
                 remote(
-                    sig_ref.at[pl.ds(dest * mine_n + 2 * pair, 2)],
-                    xbuf.at[pl.ds(2 * pair, 2), :, pl.ds(here * piece, piece)],
-                    sig_send.at[pair, j],
-                    sig_recv.at[pair, j],
+                    outside(sig, dest, which),
+                    inside(xbuf, here, which),
+                    sig_send.at[which, j],
+                    sig_recv.at[which, j],
                     where,
                 )
                 for j, (dest, where) in enumerate(peers)
+                for which in (2 * pair, 2 * pair + 1)
             ]
         )
-    for pair in range(pairs):
+    for which in range(mine_n):
         keep = pltpu.make_async_copy(
-            sig_ref.at[pl.ds(here * mine_n + 2 * pair, 2)],
-            xbuf.at[pl.ds(2 * pair, 2), :, pl.ds(here * piece, piece)],
-            own_sem.at[pair],
+            outside(sig, here, which), inside(xbuf, here, which), own_sem.at[which]
         )
         keep.start()
         own.append(keep)
@@ -317,9 +357,23 @@
     for copy in tap_copies:
         copy.wait_recv()
     spread_copies = [
-        remote(hbuf.at[:, :, chan], hbuf.at[:, :, chan], spread_send.at[j], spread_recv.at[j], where)
+        remote(hbuf.at[:, chan], hbuf.at[:, chan], spread_send.at[j], spread_recv.at[j], where)
         for j, where in enumerate(sides)
     ]
+
+    square = (chans, chans)
+    diagonal = lax.broadcasted_iota(jnp.int32, square, 0) == lax.broadcasted_iota(jnp.int32, square, 1)
+    skips = jnp.sum(
+        jnp.where(diagonal, jnp.broadcast_to(skip_ref[...], square), 0.0), axis=1, keepdims=True
+    )
+
+    def direct_step(t, carry):
+        lanes = pl.ds(pl.multiple_of(t * LANES, LANES), LANES)
+        prod = key[:, lanes].astype(jnp.float32) * value[:, lanes].astype(jnp.float32)
+        out_ref[:, lanes] = skips * prod
+        return carry
+
+    lax.fori_loop(0, tiles, direct_step, 0, unroll=4)
     for copy in tables:
         copy.wait()
     for copy in spread_copies:
@@ -348,7 +402,10 @@
         turned = jnp.concatenate(turn_forward(real, imag, cos_t, sine_t), axis=1)
         return dot3(*split(turned), col[0], col[1])
 
-    fill(lambda half: hbuf[half].reshape(rows, LANES), None)
+    tap_rows = hbuf.shape[2]
+    fill(
+        lambda half: hbuf[:, :, pl.ds(half, tap_rows // 2, stride=2), :].reshape(rows, LANES), None
+    )
 
     def filter_step(t, carry):
         at = pl.ds(pl.multiple_of(t * step, step), step)
@@ -359,10 +416,15 @@
 
     out_copies = []
     for pair in range(pairs):
-        own[1 + pair].wait()
+        own[1 + 2 * pair].wait()
+        own[2 + 2 * pair].wait()
         for copy in sig_copies[pair]:
             copy.wait_recv()
-        fill(lambda half: xbuf[2 * pair, half], lambda half: xbuf[2 * pair + 1, half])
+
+        def part(which):
+            return lambda half: xbuf[pl.ds(which * freqs + half, rows, stride=2), :]
+
+        fill(part(2 * pair), part(2 * pair + 1))
 
         def pair_step(t, carry):
             at = pl.ds(pl.multiple_of(t * step, step), step)
@@ -393,33 +455,50 @@
         for which in range(2):
             for half in range(2):
                 first = which * COLS + half * LANES
-                ybuf[2 * pair + which, half] = result[:, first : first + LANES]
+                place = pl.ds((2 * pair + which) * freqs + half, rows, stride=2)
+                ybuf[place, :] = result[:, first : first + LANES]
         out_copies.append(
             [
                 remote(
-                    ybuf.at[pl.ds(2 * pair, 2), :, pl.ds(dest * piece, piece)],
-                    conv_ref.at[pl.ds(here * mine_n + 2 * pair, 2)],
-                    out_send.at[pair, j],
-                    out_recv.at[pair, j],
+                    inside(ybuf, dest, which),
+                    outside(conv, here, which),
+                    out_send.at[which, j],
+                    out_recv.at[which, j],
                     where,
                 )
                 for j, (dest, where) in enumerate(peers)
+                for which in (2 * pair, 2 * pair + 1)
             ]
         )
-        keep = pltpu.make_async_copy(
-            ybuf.at[pl.ds(2 * pair, 2), :, pl.ds(here * piece, piece)],
-            conv_ref.at[pl.ds(here * mine_n + 2 * pair, 2)],
-            own_sem.at[pairs + pair],
-        )
-        keep.start()
-        own.append(keep)
-
-    for pair in range(pairs):
-        own[1 + pairs + pair].wait()
-        for copy in out_copies[pair]:
-            copy.wait_recv()
+        for which in (2 * pair, 2 * pair + 1):
+            keep = pltpu.make_async_copy(
+                inside(ybuf, here, which), outside(conv, here, which), own_sem.at[mine_n + which]
+            )
+            keep.start()
+            own.append(keep)
+
+    loads[2].wait()
+    for copy in own[1 + mine_n :]:
+        copy.wait()
+    for copy in sum(out_copies, []):
+        copy.wait_recv()
+
+    def gate_step(t, carry):
+        lanes = pl.ds(pl.multiple_of(t * LANES, LANES), LANES)
+        gates = gate[:, lanes].astype(jnp.float32)
+        for k in range(chans // 8):
+            at = pl.ds(8 * k, 8)
+            mixed = conv[pl.ds(8 * k * tiles + t, 8, stride=tiles), :] + out_ref[at, lanes]
+            out_ref[at, lanes] = gates[8 * k : 8 * k + 8] * mixed
+        return carry
+
+    lax.fori_loop(0, tiles, gate_step, 0, unroll=8)
     for copy in tap_copies + spread_copies + sum(sig_copies, []) + sum(out_copies, []):
         copy.wait_send()
+
+
+def keep_hbm(array):
+    return pltpu.with_memory_space_constraint(array, pltpu.HBM)
 
 
 def local_whole(gate_proj, key_proj, value_proj, filter_taps, skip_gain):
@@ -427,26 +506,26 @@
     groups = sizes[0] * sizes[1]
     chans, tok_local = gate_proj.shape
     mine_n = chans // groups
-    pairs = mine_n // 2
-    piece = tok_local // COLS
-    rows = groups * piece
-    tap_rows = filter_taps.shape[0] // COLS
-    signal = key_proj.astype(jnp.float32) * value_proj.astype(jnp.float32)
-    sig_in = signal.reshape(chans, piece, 2, LANES).transpose(0, 2, 1, 3)
-    tap_in = filter_taps.reshape(tap_rows, 2, LANES).transpose(1, 0, 2)
+    rows = groups * tok_local // COLS
+    tap_rows = filter_taps.shape[0] // LANES
     dma = pltpu.SemaphoreType.DMA
     vmem = pl.BlockSpec(memory_space=pltpu.VMEM)
-    hbm = pl.BlockSpec(memory_space=pl.ANY)
+    hbm = pl.BlockSpec(memory_space=pltpu.HBM)
     tables = dft_tables(rows)
-    conv = pl.pallas_call(
+    return pl.pallas_call(
         functools.partial(conv_kernel, sizes),
-        out_shape=jax.ShapeDtypeStruct((chans, 2, piece, LANES), jnp.float32),
-        in_specs=[vmem, vmem, hbm, hbm, hbm, hbm],
+        out_shape=jax.ShapeDtypeStruct((chans, tok_local), jnp.float32),
+        in_specs=[hbm, hbm, hbm, vmem, vmem, hbm, hbm, hbm, hbm],
         out_specs=vmem,
         scratch_shapes=[
-            pltpu.VMEM((mine_n, 2, rows, LANES), jnp.float32),
-            pltpu.VMEM((2, groups, sizes[2], tap_rows, LANES), jnp.float32),
-            pltpu.VMEM((mine_n, 2, rows, LANES), jnp.float32),
+            pltpu.VMEM((chans, tok_local), gate_proj.dtype),
+            pltpu.VMEM((chans, tok_local), key_proj.dtype),
+            pltpu.VMEM((chans, tok_local), value_proj.dtype),
+            pltpu.VMEM((chans * tok_local // LANES, LANES), jnp.float32),
+            pltpu.VMEM((chans * tok_local // LANES, LANES), jnp.float32),
+            pltpu.VMEM((mine_n * 2 * rows, LANES), jnp.float32),
+            pltpu.VMEM((groups, sizes[2], tap_rows, LANES), jnp.float32),
+            pltpu.VMEM((mine_n * 2 * rows, LANES), jnp.float32),
             pltpu.VMEM((2, 2 * rows, 2 * COLS), jnp.bfloat16),
             pltpu.VMEM((2, 4 * rows, 2 * COLS), jnp.bfloat16),
             pltpu.VMEM((2 * rows, 2 * COLS), jnp.float32),
@@ -454,29 +533,40 @@
             pltpu.VMEM(tables[1].shape, jnp.bfloat16),
             pltpu.VMEM(tables[2].shape, jnp.bfloat16),
             pltpu.VMEM(tables[3].shape, jnp.float32),
-            dma((pairs, groups - 1)),
-            dma((pairs, groups - 1)),
-            dma((pairs, groups - 1)),
-            dma((pairs, groups - 1)),
+            dma((mine_n, groups - 1)),
+            dma((mine_n, groups - 1)),
+            dma((mine_n, groups - 1)),
+            dma((mine_n, groups - 1)),
             dma((groups - 1,)),
             dma((groups - 1,)),
             dma((sizes[2] - 1,)),
             dma((sizes[2] - 1,)),
-            dma((2 * pairs + 1,)),
+            dma((2 * mine_n + 1,)),
             dma((4,)),
+            dma((3,)),
         ],
         compiler_params=pltpu.CompilerParams(
             collective_id=0, has_side_effects=True, vmem_limit_bytes=48 * 1024 * 1024
         ),
-    )(sig_in, tap_in, *(jnp.asarray(table) for table in tables))
-    conv = conv.transpose(0, 2, 1, 3).reshape(chans, tok_local)
-    return gate_proj.astype(jnp.float32) * (conv + skip_gain[:, None] * signal)
+    )(
+        keep_hbm(gate_proj),
+        keep_hbm(key_proj),
+        keep_hbm(value_proj),
+        keep_hbm(filter_taps.reshape(tap_rows, LANES)),
+        keep_hbm(skip_gain[None, :]),
+        *(keep_hbm(jnp.asarray(table)) for table in tables),
+    )
+
+
+def power_of_two(number):
+    return number & (number - 1) == 0
 
 
 def local(gate_proj, key_proj, value_proj, filter_taps, skip_gain):
     groups = lax.axis_size("outer") * lax.axis_size("inner")
     whole_pairs = gate_proj.shape[0] % (2 * groups) == 0
-    tiled = gate_proj.shape[1] % (8 * COLS) == 0 and filter_taps.shape[0] % (8 * COLS) == 0
+    flips = all(power_of_two(lax.axis_size(name)) for name in ("outer", "inner", "chan"))
+    tiled = flips and gate_proj.shape[1] % (8 * COLS) == 0 and filter_taps.shape[0] % (8 * COLS) == 0
     one = local_whole if whole_pairs and tiled else local_columns
     return one(gate_proj, key_proj, value_proj, filter_taps, skip_gain)
 

time: 61.8 us -> 57.8 us (0.935)
  local copies, waits for them, and re-layouts: 5.2 us -> 0.97 us
  Pallas kernels: 52.6 us -> 56.6 us
  other arithmetic: 3.57 us -> 0 us
    pallas_call x1, Pallas kernels: 52.6 us -> 56.6 us  [local_whole(): pl.pallas_call(functools.partial(conv_kernel, sizes), out_shape=jax.Shape...]
    mul x2 -> x0, other arithmetic: 3.57 us -> none  [the longest x1 2.27 us: local_whole(): return gate_proj.astype(jnp.float32) * (conv + skip_gain[:, None] * signal)]
    reshape x4 -> x0, local copies, waits for them, and re-layouts: 2.55 us -> none  [the longest x2 1.01 us: local_whole(): sig_in = signal.reshape(chans, piece, 2, LANES).transpose(0, 2, 1, 3)]
    unnamed x12 -> x1, local copies, waits for them, and re-layouts: 1.81 us -> 0.97 us
    transpose x1 -> x0, local copies, waits for them, and re-layouts: 0.84 us -> none  [local_whole(): conv = conv.transpose(0, 2, 1, 3).reshape(chans, tok_local)]
where the time goes in v1:
time: 57.8 us; the launch traced here: 57.6 us
  Pallas kernels  56.6 us (98%)
  local copies, waits for them, and re-layouts  0.97 us (2%)
    pallas_call x1, Pallas kernels, local_whole(): pl.pallas_call(functools.partial(conv_kernel, sizes), out_shape=jax.Shape...  56.6 us

profile of v1, /device:TPU:0, one launch (start us, length us, event | category | flops | bytes accessed | tf_op | source)
XLA Modules:
  0.0 57.6 jit_solution(18294889933688839671)
XLA Ops:
  0.0 56.6 %shard_map.91 = f32[32,8192]{1,0:T(8,128)S(1)} custom-call(bf16[32,8192]{1,0:T(8,128)(2,1)} %gate_hbm.1, bf16[32,8192]{1,0:T(8,128)(2,1)} %key_hbm.1, bf16[32,8192]{1,0:T(8,128)(2,1)} %value_hbm.1, f32[16,128]{1,0:T(8,128)} %bitcast.2, f32[1,32]{1,0:T(1,128)} %bitcast.3, bf16[2,512,512]{2,1,0:T(8,128)(2,1)} %constant.8.clone.fwd_hbm, ...), custom_call_target="tpu_custom_call" | custom-call | tf_op jit(solution)/shard_map/pallas_call | solution.py:515
  56.6 1.0 %copy.11 = f32[32,8192]{1,0:T(8,128)} copy(f32[32,8192]{1,0:T(8,128)S(1)} %shard_map.91) | data formatting | bytes 2097152

commit v2 on v1

--- a/solution.py
+++ b/solution.py
@@ -251,12 +251,14 @@
     own_sem,
     table_sem,
     load_sem,
+    skip_buf,
 ):
     outer_n, inner_n, chan_n = sizes
     groups = outer_n * inner_n
     chans, tok_local = out_ref.shape
     tiles = tok_local // LANES
     mine_n = chans // groups
+    plane = inner_n * mine_n
     pairs = mine_n // 2
     rows = groups * tiles // 2
     freqs = 2 * rows
@@ -265,7 +267,9 @@
     inner = lax.axis_index("inner")
     chan = lax.axis_index("chan")
     here = outer * inner_n + inner
-    hops = [(dz, dx) for dz in range(outer_n)[::-1] for dx in range(inner_n)[::-1] if dz or dx]
+    order = range(outer_n)[::-1]
+    firsts = [pl.multiple_of(flip(outer, dz) * plane, 8) for dz in order]
+    hops = [(dz, dx) for dz in order for dx in range(inner_n)[::-1] if dz or dx]
     peers = []
     for dz, dx in hops:
         to_z, to_x = flip(outer, dz), flip(inner, dx)
@@ -279,22 +283,30 @@
         pl.semaphore_signal(barrier, inc=1, device_id=where, device_id_type=MESH)
 
     loads = [
-        pltpu.make_async_copy(src, dst, load_sem.at[k])
-        for k, (src, dst) in enumerate(((key_hbm, key), (value_hbm, value), (gate_hbm, gate)))
+        pltpu.make_async_copy(src.at[pl.ds(firsts[i], plane)], dst.at[i], load_sem.at[i, k])
+        for i in range(outer_n)
+        for k, (src, dst) in enumerate(((key_hbm, key), (value_hbm, value)))
     ]
     for copy in loads:
         copy.start()
-    loads[0].wait()
-    loads[1].wait()
-
-    def product_step(t, carry):
-        lanes = pl.ds(pl.multiple_of(t * LANES, LANES), LANES)
-        prod = key[:, lanes].astype(jnp.float32) * value[:, lanes].astype(jnp.float32)
-        for k in range(chans // 8):
-            sig[pl.ds(8 * k * tiles + t, 8, stride=tiles), :] = prod[8 * k : 8 * k + 8]
-        return carry
-
-    lax.fori_loop(0, tiles, product_step, 0, unroll=8)
+
+    def product(i, lanes):
+        return key[i, :, lanes].astype(jnp.float32) * value[i, :, lanes].astype(jnp.float32)
+
+    def make_signal(i):
+        loads[2 * i].wait()
+        loads[2 * i + 1].wait()
+
+        def product_step(t, carry):
+            prod = product(i, pl.ds(pl.multiple_of(t * LANES, LANES), LANES))
+            for k in range(plane // 8):
+                start = (firsts[i] + 8 * k) * tiles + t
+                sig[pl.ds(start, 8, stride=tiles), :] = prod[8 * k : 8 * k + 8]
+            return carry
+
+        lax.fori_loop(0, tiles, product_step, 0, unroll=8)
+
+    make_signal(0)
     pl.semaphore_wait(barrier, len(peers) + len(sides))
 
     def remote(src, dst, send, recv, where):
@@ -323,21 +335,29 @@
     ]
     own = [pltpu.make_async_copy(tap_ref, hbuf.at[here, chan], own_sem.at[2 * mine_n])]
     own[0].start()
-    sig_copies = []
-    for pair in range(pairs):
-        sig_copies.append(
-            [
-                remote(
-                    outside(sig, dest, which),
-                    inside(xbuf, here, which),
-                    sig_send.at[which, j],
-                    sig_recv.at[which, j],
-                    where,
-                )
-                for j, (dest, where) in enumerate(peers)
-                for which in (2 * pair, 2 * pair + 1)
-            ]
-        )
+    sig_copies = [[] for _ in range(pairs)]
+
+    def send_signal(i, pair):
+        for j, (dest, where) in enumerate(peers):
+            if hops[j][0] == order[i]:
+                for which in (2 * pair, 2 * pair + 1):
+                    sig_copies[pair].append(
+                        remote(
+                            outside(sig, dest, which),
+                            inside(xbuf, here, which),
+                            sig_send.at[which, j],
+                            sig_recv.at[which, j],
+                            where,
+                        )
+                    )
+
+    for i in range(outer_n):
+        if i:
+            make_signal(i)
+        send_signal(i, 0)
+    for pair in range(1, pairs):
+        for i in range(outer_n):
+            send_signal(i, pair)
     for which in range(mine_n):
         keep = pltpu.make_async_copy(
             outside(sig, here, which), inside(xbuf, here, which), own_sem.at[which]
@@ -350,7 +370,13 @@
             ((fwd_hbm, fwd), (col_hbm, col), (twid_hbm, twid), (inv_hbm, inv))
         )
     ]
-    for copy in tables:
+    gates = [
+        pltpu.make_async_copy(
+            gate_hbm.at[pl.ds(firsts[i], plane)], gate.at[i], load_sem.at[i, 2]
+        )
+        for i in range(outer_n)
+    ]
+    for copy in tables + gates:
         copy.start()
 
     own[0].wait()
@@ -367,10 +393,13 @@
         jnp.where(diagonal, jnp.broadcast_to(skip_ref[...], square), 0.0), axis=1, keepdims=True
     )
 
+    skip_buf[...] = jnp.broadcast_to(skips, (chans, LANES))
+
     def direct_step(t, carry):
         lanes = pl.ds(pl.multiple_of(t * LANES, LANES), LANES)
-        prod = key[:, lanes].astype(jnp.float32) * value[:, lanes].astype(jnp.float32)
-        out_ref[:, lanes] = skips * prod
+        for i in range(outer_n):
+            at = pl.ds(firsts[i], plane)
+            out_ref[at, lanes] = skip_buf[at, :] * product(i, lanes)
         return carry
 
     lax.fori_loop(0, tiles, direct_step, 0, unroll=4)
@@ -477,22 +506,29 @@
             keep.start()
             own.append(keep)
 
-    loads[2].wait()
-    for copy in own[1 + mine_n :]:
-        copy.wait()
-    for copy in sum(out_copies, []):
-        copy.wait_recv()
-
-    def gate_step(t, carry):
-        lanes = pl.ds(pl.multiple_of(t * LANES, LANES), LANES)
-        gates = gate[:, lanes].astype(jnp.float32)
-        for k in range(chans // 8):
-            at = pl.ds(8 * k, 8)
-            mixed = conv[pl.ds(8 * k * tiles + t, 8, stride=tiles), :] + out_ref[at, lanes]
-            out_ref[at, lanes] = gates[8 * k : 8 * k + 8] * mixed
-        return carry
-
-    lax.fori_loop(0, tiles, gate_step, 0, unroll=8)
+    def gate_plane(i):
+        def gate_step(t, carry):
+            lanes = pl.ds(pl.multiple_of(t * LANES, LANES), LANES)
+            factor = gate[i, :, lanes].astype(jnp.float32)
+            for k in range(plane // 8):
+                at = pl.ds(pl.multiple_of(firsts[i] + 8 * k, 8), 8)
+                start = (firsts[i] + 8 * k) * tiles + t
+                mixed = conv[pl.ds(start, 8, stride=tiles), :] + out_ref[at, lanes]
+                out_ref[at, lanes] = factor[8 * k : 8 * k + 8] * mixed
+            return carry
+
+        lax.fori_loop(0, tiles, gate_step, 0, unroll=8)
+
+    for i in reversed(range(outer_n)):
+        gates[i].wait()
+        if order[i] == 0:
+            for copy in own[1 + mine_n :]:
+                copy.wait()
+        for pair in range(pairs):
+            for n, copy in enumerate(out_copies[pair]):
+                if hops[n // 2][0] == order[i]:
+                    copy.wait_recv()
+        gate_plane(i)
     for copy in tap_copies + spread_copies + sum(sig_copies, []) + sum(out_copies, []):
         copy.wait_send()
 
@@ -518,9 +554,9 @@
         in_specs=[hbm, hbm, hbm, vmem, vmem, hbm, hbm, hbm, hbm],
         out_specs=vmem,
         scratch_shapes=[
-            pltpu.VMEM((chans, tok_local), gate_proj.dtype),
-            pltpu.VMEM((chans, tok_local), key_proj.dtype),
-            pltpu.VMEM((chans, tok_local), value_proj.dtype),
+            pltpu.VMEM((sizes[0], chans // sizes[0], tok_local), gate_proj.dtype),
+            pltpu.VMEM((sizes[0], chans // sizes[0], tok_local), key_proj.dtype),
+            pltpu.VMEM((sizes[0], chans // sizes[0], tok_local), value_proj.dtype),
             pltpu.VMEM((chans * tok_local // LANES, LANES), jnp.float32),
             pltpu.VMEM((chans * tok_local // LANES, LANES), jnp.float32),
             pltpu.VMEM((mine_n * 2 * rows, LANES), jnp.float32),
@@ -543,7 +579,8 @@
             dma((sizes[2] - 1,)),
             dma((2 * mine_n + 1,)),
             dma((4,)),
-            dma((3,)),
+            dma((sizes[0], 3)),
+            pltpu.VMEM((chans, LANES), jnp.float32),
         ],
         compiler_params=pltpu.CompilerParams(
             collective_id=0, has_side_effects=True, vmem_limit_bytes=48 * 1024 * 1024
@@ -567,6 +604,7 @@
     whole_pairs = gate_proj.shape[0] % (2 * groups) == 0
     flips = all(power_of_two(lax.axis_size(name)) for name in ("outer", "inner", "chan"))
     tiled = flips and gate_proj.shape[1] % (8 * COLS) == 0 and filter_taps.shape[0] % (8 * COLS) == 0
+    tiled = tiled and gate_proj.shape[0] // lax.axis_size("outer") % 8 == 0
     one = local_whole if whole_pairs and tiled else local_columns
     return one(gate_proj, key_proj, value_proj, filter_taps, skip_gain)
 

time: 57.8 us -> 57.4 us (level)
  no operation moved by 1% of the time
where the time goes in v2:
time: 57.4 us; the launch traced here: 57.2 us
  Pallas kernels  56.2 us (98%)
  local copies, waits for them, and re-layouts  0.97 us (2%)
    pallas_call x1, Pallas kernels, local_whole(): pl.pallas_call(functools.partial(conv_kernel, sizes), out_shape=jax.Shape...  56.2 us

profile of v2, /device:TPU:0, one launch (start us, length us, event | category | flops | bytes accessed | tf_op | source)
XLA Modules:
  0.0 57.2 jit_solution(9288443484143192597)
XLA Ops:
  0.0 56.2 %shard_map.91 = f32[32,8192]{1,0:T(8,128)S(1)} custom-call(bf16[32,8192]{1,0:T(8,128)(2,1)} %gate_hbm.1, bf16[32,8192]{1,0:T(8,128)(2,1)} %key_hbm.1, bf16[32,8192]{1,0:T(8,128)(2,1)} %value_hbm.1, f32[16,128]{1,0:T(8,128)} %bitcast.2, f32[1,32]{1,0:T(1,128)} %bitcast.3, bf16[2,512,512]{2,1,0:T(8,128)(2,1)} %constant.8.clone.fwd_hbm, ...), custom_call_target="tpu_custom_call" | custom-call | tf_op jit(solution)/shard_map/pallas_call | solution.py:551
  56.2 1.0 %copy.11 = f32[32,8192]{1,0:T(8,128)} copy(f32[32,8192]{1,0:T(8,128)S(1)} %shard_map.91) | data formatting | bytes 2097152
